TPU v7x, 128 devices: a whole 4x4x4 slice. The times are simulated.
128 devices in a mesh: row: 8 (over z, y_hi), col: 4 (over y_lo, core), feat: 4 (over x).
Axes of the slice: x: 4, y: 4 (y_hi: 2, y_lo: 2; y = y_hi * 2 + y_lo), z: 4, core: 2. Of those that a mesh axis runs over, the one named last changes fastest.
Arguments:
- features: bfloat16 [262144, 128], P(('row', 'col'), 'feat'), may hold values from -6 to 6
- tiles: bfloat16 [8, 4, 1536, 128, 128], P('row', 'col', 'feat'), may hold values from 0 to 0.04321289
- tile_row: int32 [8, 4, 1536], P('row', 'col', 'feat'), may hold values from 0 to 255
- tile_col: int32 [8, 4, 1536], P('row', 'col', 'feat'), may hold values from 0 to 511
- tile_count: int32 [8, 4, 4], P('row', 'col', 'feat'), may hold values from 1 to 384, as said below
- weight: bfloat16 [128, 256], replicated, may hold values from -0.5 to 0.5
- bias: float32 [256], replicated, may hold values from -3 to 3
Outputs:
- output: bfloat16 [262144, 256], P(('row', 'col', 'feat'))
Inputs may be any that keep to these rules, and one draw needn't show every extreme that they name: `tile_count`: some device has all 384 slots live.
All inputs are finite; a program needn't handle non-finite values.
Results may differ from a plain program's by a relative error of at most 0.02.
Values may be sent and summed in bfloat16 or wider, within the bound.
No kernel may reach another device: no remote copies, remote signals or barrier semaphores. Data moves between devices by JAX's collectives and lax.ppermute only.
A program may use at most 128 MiB of HBM per device.

v0:
```python
import jax
import jax.numpy as jnp
from jax import lax
from jax.sharding import PartitionSpec as P


def body(features, tiles, tile_row, tile_col, tile_count, weight, bias):
    node_rows = lax.all_to_all(features, "feat", split_axis=0, concat_axis=1, tiled=True)
    sources = lax.all_gather(node_rows, ("row", "feat"), axis=0, tiled=True)
    tile_side = tiles.shape[-1]
    width = sources.shape[1]
    node_dev = features.shape[0] // lax.axis_size("feat")
    block_rows = lax.axis_size("col") * lax.axis_size("feat") * node_dev // tile_side
    src_blocks = sources.reshape(-1, tile_side, width)
    slot_total = tiles.shape[2]
    tile_stack = tiles.reshape(slot_total, tile_side, tile_side)
    row_index = tile_row.reshape(slot_total)
    col_index = tile_col.reshape(slot_total)
    live_count = tile_count.reshape(())
    block = min(32, slot_total)
    turns = (live_count + block - 1) // block

    def one_turn(turn, partial_value):
        start = turn * block
        tile_block = lax.dynamic_slice_in_dim(tile_stack, start, block, 0)
        rows_here = lax.dynamic_slice_in_dim(row_index, start, block, 0)
        cols_here = lax.dynamic_slice_in_dim(col_index, start, block, 0)
        picked = jnp.take(src_blocks, cols_here, axis=0)
        prods = jnp.einsum("tij,tjf->tif", tile_block, picked, preferred_element_type=jnp.float32)
        live = start + jnp.arange(block, dtype=jnp.int32) < live_count
        prods = jnp.where(live[:, None, None], prods, jnp.zeros_like(prods))
        return partial_value.at[rows_here].add(prods)

    empty = jnp.zeros((block_rows, tile_side, width), jnp.float32)
    partial_value = lax.fori_loop(0, turns, one_turn, empty)
    rounded = lax.optimization_barrier(
        partial_value.reshape(block_rows * tile_side, width).astype(jnp.bfloat16)
    )
    terms = rounded.astype(jnp.float32)
    agg = lax.psum_scatter(
        terms.astype(jnp.bfloat16), ("col", "feat"), scatter_dimension=0, tiled=True
    )
    hidden = jnp.dot(agg, weight, preferred_element_type=jnp.float32) + bias
    return jax.nn.relu(hidden).astype(jnp.bfloat16)


def solution(mesh):
    placed = (
        P(("row", "col"), "feat"),
        P("row", "col", "feat", None, None),
        P("row", "col", "feat"),
        P("row", "col", "feat"),
        P("row", "col", "feat"),
        P(),
        P(),
    )
    return jax.shard_map(
        body, mesh=mesh, in_specs=placed, out_specs=P(("row", "col", "feat"), None), check_vma=False
    )
```

profile of v0, /device:TPU:1, one launch (start us, length us, event | category | flops | bytes accessed | tf_op | source)
XLA Modules:
  0.0 501.4 jit_solution(782019901176667349)
XLA Ops:
  7.7 13.3 %all_to_all.19 = bf16[4,2048,32]{1,2,0:T(8,128)(2,1)} all-to-all(bf16[4,2048,32]{1,2,0:T(8,128)(2,1)S(1)} %bitcast.18), channel_id=1, replica_groups=mesh['row'=8,'col'=4,'feat'=4] {'feat'}, dimensions={0} | all-to-all | bytes 1048576 | tf_op jit(solution)/shard_map/all_to_all | solution.py:8
  23.1 150.9 %all-gather.2.cloned.1.call-done = bf16[65536,128]{0,1:T(8,128)(2,1)} async-done(((bf16[2048,128]{0,1:T(8,128)(2,1)}), bf16[65536,128]{0,1:T(8,128)(2,1)}) %all-gather.2.cloned.1.call-update) | async-done | bytes 16777232 | tf_op jit(solution)/shard_map/all_gather | solution.py:9
  174.0 22.4 %copy.14 = bf16[65536,128]{1,0:T(8,128)(2,1)} copy(bf16[65536,128]{0,1:T(8,128)(2,1)} %all-gather.2.cloned.1.call-done) | data formatting | bytes 33554432 | tf_op jit(solution)/shard_map/while | solution.py:35
  196.4 7.8 %broadcast_in_dim.28 = f32[256,128,128]{2,1,0:T(8,128)} broadcast(f32[]{:T(128)} %constant.47.clone.1), dimensions={} | broadcast | bytes 16777220 | tf_op jit(solution)/shard_map/broadcast_in_dim | solution.py:34
  204.3 106.8 %while.10 = (s32[]{:T(128)}, f32[256,128,128]{2,1,0:T(8,128)}, s32[]{:T(128)}, s32[384]{0:T(512)S(1)}, s32[]{:T(128)}, /*index=5*/bf16[384,128,128]{2,1,0:T(8,12...) while((s32[]{:T(128)}, f32[256,128,128]{2,1,0:T(8,128)}, ...), condition=%wide.region_2.3_spmd, body=%wide.region_0.2_spmd.sunk | while | flops 135791968 | bytes 12588215 | solution.py:35
  205.1 6.5 %gather_fusion = bf16[32,128,128]{2,1,0:T(8,128)(2,1)S(1)} fusion(bf16[512,128,128]{2,1,0:T(8,128)(2,1)} %get-tuple-element.179, s32[1024]{0:T(1024)S(1)} %pad_clamp_fusion.2), kind=kCustom, calls=%fused_computation.clone.1 | custom fusion | bytes 2097280 | tf_op jit(solution)/shard_map/while/body/jit(_take)/gather | solution.py:28
  213.4 6.2 %scatter_fusion = f32[256,128,128]{2,1,0:T(8,128)} fusion(f32[256,128,128]{2,1,0:T(8,128)} %get-tuple-element.161, s32[32]{0:T(128)S(1)} %compare_select_fusion.4, f32[32,128,128]{2,1,0:T(8,128)S(1)} %convolution_select_fusion.2), kind=kCustom, calls=%fused_computation.1.clone.1 | custom fusion | flops 524288 | bytes 6291584 | tf_op jit(solution)/shard_map/while/body/scatter-add | solution.py:32
  220.4 6.5 %gather_fusion = bf16[32,128,128]{2,1,0:T(8,128)(2,1)S(1)} fusion(bf16[512,128,128]{2,1,0:T(8,128)(2,1)} %get-tuple-element.179, s32[1024]{0:T(1024)S(1)} %pad_clamp_fusion.2), kind=kCustom, calls=%fused_computation.clone.1 | custom fusion | bytes 2097280 | tf_op jit(solution)/shard_map/while/body/jit(_take)/gather | solution.py:28
  226.9 1.7 convolution_select_fusion.2
  228.7 6.2 %scatter_fusion = f32[256,128,128]{2,1,0:T(8,128)} fusion(f32[256,128,128]{2,1,0:T(8,128)} %get-tuple-element.161, s32[32]{0:T(128)S(1)} %compare_select_fusion.4, f32[32,128,128]{2,1,0:T(8,128)S(1)} %convolution_select_fusion.2), kind=kCustom, calls=%fused_computation.1.clone.1 | custom fusion | flops 524288 | bytes 6291584 | tf_op jit(solution)/shard_map/while/body/scatter-add | solution.py:32
  235.7 6.5 %gather_fusion = bf16[32,128,128]{2,1,0:T(8,128)(2,1)S(1)} fusion(bf16[512,128,128]{2,1,0:T(8,128)(2,1)} %get-tuple-element.179, s32[1024]{0:T(1024)S(1)} %pad_clamp_fusion.2), kind=kCustom, calls=%fused_computation.clone.1 | custom fusion | bytes 2097280 | tf_op jit(solution)/shard_map/while/body/jit(_take)/gather | solution.py:28
  244.0 6.1 %scatter_fusion = f32[256,128,128]{2,1,0:T(8,128)} fusion(f32[256,128,128]{2,1,0:T(8,128)} %get-tuple-element.161, s32[32]{0:T(128)S(1)} %compare_select_fusion.4, f32[32,128,128]{2,1,0:T(8,128)S(1)} %convolution_select_fusion.2), kind=kCustom, calls=%fused_computation.1.clone.1 | custom fusion | flops 524288 | bytes 6291584 | tf_op jit(solution)/shard_map/while/body/scatter-add | solution.py:32
  250.9 6.5 %gather_fusion = bf16[32,128,128]{2,1,0:T(8,128)(2,1)S(1)} fusion(bf16[512,128,128]{2,1,0:T(8,128)(2,1)} %get-tuple-element.179, s32[1024]{0:T(1024)S(1)} %pad_clamp_fusion.2), kind=kCustom, calls=%fused_computation.clone.1 | custom fusion | bytes 2097280 | tf_op jit(solution)/shard_map/while/body/jit(_take)/gather | solution.py:28
  259.2 6.2 %scatter_fusion = f32[256,128,128]{2,1,0:T(8,128)} fusion(f32[256,128,128]{2,1,0:T(8,128)} %get-tuple-element.161, s32[32]{0:T(128)S(1)} %compare_select_fusion.4, f32[32,128,128]{2,1,0:T(8,128)S(1)} %convolution_select_fusion.2), kind=kCustom, calls=%fused_computation.1.clone.1 | custom fusion | flops 524288 | bytes 6291584 | tf_op jit(solution)/shard_map/while/body/scatter-add | solution.py:32
  266.2 6.5 %gather_fusion = bf16[32,128,128]{2,1,0:T(8,128)(2,1)S(1)} fusion(bf16[512,128,128]{2,1,0:T(8,128)(2,1)} %get-tuple-element.179, s32[1024]{0:T(1024)S(1)} %pad_clamp_fusion.2), kind=kCustom, calls=%fused_computation.clone.1 | custom fusion | bytes 2097280 | tf_op jit(solution)/shard_map/while/body/jit(_take)/gather | solution.py:28
  274.5 6.2 %scatter_fusion = f32[256,128,128]{2,1,0:T(8,128)} fusion(f32[256,128,128]{2,1,0:T(8,128)} %get-tuple-element.161, s32[32]{0:T(128)S(1)} %compare_select_fusion.4, f32[32,128,128]{2,1,0:T(8,128)S(1)} %convolution_select_fusion.2), kind=kCustom, calls=%fused_computation.1.clone.1 | custom fusion | flops 524288 | bytes 6291584 | tf_op jit(solution)/shard_map/while/body/scatter-add | solution.py:32
  281.5 6.5 %gather_fusion = bf16[32,128,128]{2,1,0:T(8,128)(2,1)S(1)} fusion(bf16[512,128,128]{2,1,0:T(8,128)(2,1)} %get-tuple-element.179, s32[1024]{0:T(1024)S(1)} %pad_clamp_fusion.2), kind=kCustom, calls=%fused_computation.clone.1 | custom fusion | bytes 2097280 | tf_op jit(solution)/shard_map/while/body/jit(_take)/gather | solution.py:28
  288.0 1.7 convolution_select_fusion.2
  289.8 6.1 %scatter_fusion = f32[256,128,128]{2,1,0:T(8,128)} fusion(f32[256,128,128]{2,1,0:T(8,128)} %get-tuple-element.161, s32[32]{0:T(128)S(1)} %compare_select_fusion.4, f32[32,128,128]{2,1,0:T(8,128)S(1)} %convolution_select_fusion.2), kind=kCustom, calls=%fused_computation.1.clone.1 | custom fusion | flops 524288 | bytes 6291584 | tf_op jit(solution)/shard_map/while/body/scatter-add | solution.py:32
  296.7 6.5 %gather_fusion = bf16[32,128,128]{2,1,0:T(8,128)(2,1)S(1)} fusion(bf16[512,128,128]{2,1,0:T(8,128)(2,1)} %get-tuple-element.179, s32[1024]{0:T(1024)S(1)} %pad_clamp_fusion.2), kind=kCustom, calls=%fused_computation.clone.1 | custom fusion | bytes 2097280 | tf_op jit(solution)/shard_map/while/body/jit(_take)/gather | solution.py:28
  305.0 6.1 %scatter_fusion = f32[256,128,128]{2,1,0:T(8,128)} fusion(f32[256,128,128]{2,1,0:T(8,128)} %get-tuple-element.161, s32[32]{0:T(128)S(1)} %compare_select_fusion.4, f32[32,128,128]{2,1,0:T(8,128)S(1)} %convolution_select_fusion.2), kind=kCustom, calls=%fused_computation.1.clone.1 | custom fusion | flops 524288 | bytes 6291584 | tf_op jit(solution)/shard_map/while/body/scatter-add | solution.py:32
  311.1 9.2 %convert_element_type.11 = bf16[256,128,128]{2,1,0:T(8,128)(2,1)} convert(f32[256,128,128]{2,1,0:T(8,128)} %get-tuple-element.48) | non-fusion elementwise | flops 4194304 | bytes 25165824 | tf_op jit(solution)/shard_map/convert_element_type | solution.py:37
  320.3 171.8 %reduce-scatter.2.cloned.1.call-done = bf16[2048,128]{1,0:T(8,128)(2,1)} async-done(((bf16[32768,128]{1,0:T(8,128)(2,1)}), bf16[2048,128]{1,0:T(8,128)(2,1)}) %reduce-scatter.2.cloned.1.call-update) | async-done | bytes 524304 | tf_op jit(solution)/shard_map/reduce_scatter | solution.py:40
  492.2 2.4 fusion.7
  (37 shorter events, 16.9 us)
Async XLA Ops:
  6.5 485.6 %copy-start = (bf16[128,256]{1,0:T(8,128)(2,1)S(1)}, bf16[128,256]{1,0:T(8,128)(2,1)}, u32[]{:S(2)}) copy-start(bf16[128,256]{1,0:T(8,128)(2,1)} %param.14) | copy-start | bytes 196612
  6.5 167.5 %all-gather.2.cloned.1.call-start = ((), (), s32[]{:S(2)}) async-start(), calls=%async_computation.2 | async-start | bytes 17301504 | tf_op jit(solution)/shard_map/all_gather | solution.py:9
  21.0 471.2 %reduce-scatter.2.cloned.1.call-start = ((), (), s32[]{:S(2)}) async-start(), calls=%async_computation.3 | async-start | bytes 8912896 | tf_op jit(solution)/shard_map/reduce_scatter | solution.py:40
  311.1 181.1 %copy-start.1 = (f32[256]{0:T(256)S(1)}, f32[256]{0:T(256)}, u32[]{:S(2)}) copy-start(f32[256]{0:T(256)} %param.15) | copy-start | bytes 3076
Sparse Core Ops, SparseCore 0:
  21.1 152.8 all-gather.1
  320.5 171.6 reduce-scatter.1
where the time goes:
time: 505 us; the launch traced here: 501 us
  waiting for transfers between devices  323 us (64%)
  local copies, waits for them, and re-layouts  77 us (15%)
  other arithmetic  59.5 us (12%)
  matrix products  14.6 us (3%)
  between operations  14.1 us (3%)
  blocking collectives  13.3 us (3%)
    reduce_scatter x1, waiting for transfers between devices, body(): lax.psum_scatter(terms.astype(jnp.bfloat16), ('col', 'feat'), scatter_dim...  172 us
    all_gather x1, waiting for transfers between devices, body(): sources = lax.all_gather(node_rows, ('row', 'feat'), axis=0, tiled=True)  151 us
    gather x7, local copies, waits for them, and re-layouts, one_turn(): picked = jnp.take(src_blocks, cols_here, axis=0)  45.6 us
    scatter-add x7, other arithmetic, one_turn(): return partial_value.at[rows_here].add(prods)  43.3 us
    while x1, local copies, waits for them, and re-layouts, body(): partial_value = lax.fori_loop(0, turns, one_turn, empty)  22.4 us
    all_to_all x1, blocking collectives, body(): lax.all_to_all(features, 'feat', split_axis=0, concat_axis=1, tiled=True)  13.3 us
    dot_general x7, matrix products, one_turn(): jnp.einsum('tij,tjf->tif', tile_block, picked, preferred_element_type=jnp...  12.2 us
  transfers between devices with their start and end apart: 2, of which 2 were waited for; matrix products, arithmetic and copies ran while one was open for 0% of the time, Pallas kernels for 0%

commit v1 on v0

--- a/solution.py
+++ b/solution.py
@@ -5,7 +5,10 @@
 
 
 def body(features, tiles, tile_row, tile_col, tile_count, weight, bias):
-    node_rows = lax.all_to_all(features, "feat", split_axis=0, concat_axis=1, tiled=True)
+    node_rows = jnp.concatenate(
+        lax.all_to_all(jnp.stack(jnp.split(features, lax.axis_size("feat"), axis=0)), "feat", 0, 0),
+        axis=1,
+    )
     sources = lax.all_gather(node_rows, ("row", "feat"), axis=0, tiled=True)
     tile_side = tiles.shape[-1]
     width = sources.shape[1]

time: 505 us -> 486 us (0.962)
  local copies, waits for them, and re-layouts: 77 us -> 55.6 us
    while x1 -> x0, local copies, waits for them, and re-layouts: 22.4 us -> none  [body(): partial_value = lax.fori_loop(0, turns, one_turn, empty)]
where the time goes in v1:
time: 486 us; the launch traced here: 484 us
  waiting for transfers between devices  326 us (67%)
  other arithmetic  59.6 us (12%)
  local copies, waits for them, and re-layouts  55.6 us (11%)
  matrix products  14.6 us (3%)
  between operations  14.1 us (3%)
  blocking collectives  13.2 us (3%)
    reduce_scatter x1, waiting for transfers between devices, body(): lax.psum_scatter(terms.astype(jnp.bfloat16), ('col', 'feat'), scatter_dim...  172 us
    all_gather x1, waiting for transfers between devices, body(): sources = lax.all_gather(node_rows, ('row', 'feat'), axis=0, tiled=True)  154 us
    gather x7, local copies, waits for them, and re-layouts, one_turn(): picked = jnp.take(src_blocks, cols_here, axis=0)  45.6 us
    scatter-add x7, other arithmetic, one_turn(): return partial_value.at[rows_here].add(prods)  43.3 us
    all_to_all x1, blocking collectives, body(): lax.all_to_all(jnp.stack(jnp.split(features, lax.axis_size('feat'), axis=...  13.2 us
    dot_general x7, matrix products, one_turn(): jnp.einsum('tij,tjf->tif', tile_block, picked, preferred_element_type=jnp...  12.2 us
  transfers between devices with their start and end apart: 2, of which 2 were waited for; matrix products, arithmetic and copies ran while one was open for 0% of the time, Pallas kernels for 0%

profile of v1, /device:TPU:1, one launch (start us, length us, event | category | flops | bytes accessed | tf_op | source)
XLA Modules:
  0.0 483.6 jit_solution(10772969125299611784)
XLA Ops:
  7.8 13.2 %all_to_all.5 = bf16[4,2048,32]{1,2,0:T(8,128)(2,1)S(1)} all-to-all(bf16[4,2048,32]{1,2,0:T(8,128)(2,1)S(1)} %pad_maximum_fusion), channel_id=1, replica_groups=mesh['row'=8,'col'=4,'feat'=4] {'feat'}, dimensions={0} | all-to-all | bytes 1048576 | tf_op jit(solution)/shard_map/all_to_all | solution.py:9
  24.1 154.5 %all-gather.2.cloned.1.call-done = bf16[65536,128]{1,0:T(8,128)(2,1)} async-done(((bf16[2048,128]{1,0:T(8,128)(2,1)}), bf16[65536,128]{1,0:T(8,128)(2,1)}) %all-gather.2.cloned.1.call-update) | async-done | bytes 16777232 | tf_op jit(solution)/shard_map/all_gather | solution.py:12
  178.6 7.8 %broadcast_in_dim.28 = f32[256,128,128]{2,1,0:T(8,128)} broadcast(f32[]{:T(128)} %constant.47.clone.1), dimensions={} | broadcast | bytes 16777220 | tf_op jit(solution)/shard_map/broadcast_in_dim | solution.py:37
  186.5 106.8 %while.10 = (s32[]{:T(128)}, f32[256,128,128]{2,1,0:T(8,128)}, s32[]{:T(128)}, s32[384]{0:T(512)S(1)}, s32[]{:T(128)}, /*index=5*/bf16[384,128,128]{2,1,0:T(8,12...) while((s32[]{:T(128)}, f32[256,128,128]{2,1,0:T(8,128)}, ...), condition=%wide.region_2.3_spmd, body=%wide.region_0.2_spmd.sunk | while | flops 135791968 | bytes 12588215 | solution.py:38
  187.3 6.5 %gather_fusion = bf16[32,128,128]{2,1,0:T(8,128)(2,1)S(1)} fusion(bf16[512,128,128]{2,1,0:T(8,128)(2,1)} %get-tuple-element.159, s32[1024]{0:T(1024)S(1)} %pad_clamp_fusion.2), kind=kCustom, calls=%fused_computation.clone.1 | custom fusion | bytes 2097280 | tf_op jit(solution)/shard_map/while/body/jit(_take)/gather | solution.py:31
  195.6 6.2 %scatter_fusion = f32[256,128,128]{2,1,0:T(8,128)} fusion(f32[256,128,128]{2,1,0:T(8,128)} %get-tuple-element.141, s32[32]{0:T(128)S(1)} %compare_select_fusion.4, f32[32,128,128]{2,1,0:T(8,128)S(1)} %convolution_select_fusion.2), kind=kCustom, calls=%fused_computation.1.clone.1 | custom fusion | flops 524288 | bytes 6291584 | tf_op jit(solution)/shard_map/while/body/scatter-add | solution.py:35
  202.6 6.5 %gather_fusion = bf16[32,128,128]{2,1,0:T(8,128)(2,1)S(1)} fusion(bf16[512,128,128]{2,1,0:T(8,128)(2,1)} %get-tuple-element.159, s32[1024]{0:T(1024)S(1)} %pad_clamp_fusion.2), kind=kCustom, calls=%fused_computation.clone.1 | custom fusion | bytes 2097280 | tf_op jit(solution)/shard_map/while/body/jit(_take)/gather | solution.py:31
  210.9 6.2 %scatter_fusion = f32[256,128,128]{2,1,0:T(8,128)} fusion(f32[256,128,128]{2,1,0:T(8,128)} %get-tuple-element.141, s32[32]{0:T(128)S(1)} %compare_select_fusion.4, f32[32,128,128]{2,1,0:T(8,128)S(1)} %convolution_select_fusion.2), kind=kCustom, calls=%fused_computation.1.clone.1 | custom fusion | flops 524288 | bytes 6291584 | tf_op jit(solution)/shard_map/while/body/scatter-add | solution.py:35
  217.9 6.5 %gather_fusion = bf16[32,128,128]{2,1,0:T(8,128)(2,1)S(1)} fusion(bf16[512,128,128]{2,1,0:T(8,128)(2,1)} %get-tuple-element.159, s32[1024]{0:T(1024)S(1)} %pad_clamp_fusion.2), kind=kCustom, calls=%fused_computation.clone.1 | custom fusion | bytes 2097280 | tf_op jit(solution)/shard_map/while/body/jit(_take)/gather | solution.py:31
  224.4 1.7 convolution_select_fusion.2
  226.2 6.1 %scatter_fusion = f32[256,128,128]{2,1,0:T(8,128)} fusion(f32[256,128,128]{2,1,0:T(8,128)} %get-tuple-element.141, s32[32]{0:T(128)S(1)} %compare_select_fusion.4, f32[32,128,128]{2,1,0:T(8,128)S(1)} %convolution_select_fusion.2), kind=kCustom, calls=%fused_computation.1.clone.1 | custom fusion | flops 524288 | bytes 6291584 | tf_op jit(solution)/shard_map/while/body/scatter-add | solution.py:35
  233.1 6.5 %gather_fusion = bf16[32,128,128]{2,1,0:T(8,128)(2,1)S(1)} fusion(bf16[512,128,128]{2,1,0:T(8,128)(2,1)} %get-tuple-element.159, s32[1024]{0:T(1024)S(1)} %pad_clamp_fusion.2), kind=kCustom, calls=%fused_computation.clone.1 | custom fusion | bytes 2097280 | tf_op jit(solution)/shard_map/while/body/jit(_take)/gather | solution.py:31
  239.6 1.7 convolution_select_fusion.2
  241.4 6.2 %scatter_fusion = f32[256,128,128]{2,1,0:T(8,128)} fusion(f32[256,128,128]{2,1,0:T(8,128)} %get-tuple-element.141, s32[32]{0:T(128)S(1)} %compare_select_fusion.4, f32[32,128,128]{2,1,0:T(8,128)S(1)} %convolution_select_fusion.2), kind=kCustom, calls=%fused_computation.1.clone.1 | custom fusion | flops 524288 | bytes 6291584 | tf_op jit(solution)/shard_map/while/body/scatter-add | solution.py:35
  248.4 6.5 %gather_fusion = bf16[32,128,128]{2,1,0:T(8,128)(2,1)S(1)} fusion(bf16[512,128,128]{2,1,0:T(8,128)(2,1)} %get-tuple-element.159, s32[1024]{0:T(1024)S(1)} %pad_clamp_fusion.2), kind=kCustom, calls=%fused_computation.clone.1 | custom fusion | bytes 2097280 | tf_op jit(solution)/shard_map/while/body/jit(_take)/gather | solution.py:31
  256.7 6.2 %scatter_fusion = f32[256,128,128]{2,1,0:T(8,128)} fusion(f32[256,128,128]{2,1,0:T(8,128)} %get-tuple-element.141, s32[32]{0:T(128)S(1)} %compare_select_fusion.4, f32[32,128,128]{2,1,0:T(8,128)S(1)} %convolution_select_fusion.2), kind=kCustom, calls=%fused_computation.1.clone.1 | custom fusion | flops 524288 | bytes 6291584 | tf_op jit(solution)/shard_map/while/body/scatter-add | solution.py:35
  263.7 6.5 %gather_fusion = bf16[32,128,128]{2,1,0:T(8,128)(2,1)S(1)} fusion(bf16[512,128,128]{2,1,0:T(8,128)(2,1)} %get-tuple-element.159, s32[1024]{0:T(1024)S(1)} %pad_clamp_fusion.2), kind=kCustom, calls=%fused_computation.clone.1 | custom fusion | bytes 2097280 | tf_op jit(solution)/shard_map/while/body/jit(_take)/gather | solution.py:31
  271.9 6.1 %scatter_fusion = f32[256,128,128]{2,1,0:T(8,128)} fusion(f32[256,128,128]{2,1,0:T(8,128)} %get-tuple-element.141, s32[32]{0:T(128)S(1)} %compare_select_fusion.4, f32[32,128,128]{2,1,0:T(8,128)S(1)} %convolution_select_fusion.2), kind=kCustom, calls=%fused_computation.1.clone.1 | custom fusion | flops 524288 | bytes 6291584 | tf_op jit(solution)/shard_map/while/body/scatter-add | solution.py:35
  278.9 6.5 %gather_fusion = bf16[32,128,128]{2,1,0:T(8,128)(2,1)S(1)} fusion(bf16[512,128,128]{2,1,0:T(8,128)(2,1)} %get-tuple-element.159, s32[1024]{0:T(1024)S(1)} %pad_clamp_fusion.2), kind=kCustom, calls=%fused_computation.clone.1 | custom fusion | bytes 2097280 | tf_op jit(solution)/shard_map/while/body/jit(_take)/gather | solution.py:31
  285.4 1.7 convolution_select_fusion.2
  287.2 6.1 %scatter_fusion = f32[256,128,128]{2,1,0:T(8,128)} fusion(f32[256,128,128]{2,1,0:T(8,128)} %get-tuple-element.141, s32[32]{0:T(128)S(1)} %compare_select_fusion.4, f32[32,128,128]{2,1,0:T(8,128)S(1)} %convolution_select_fusion.2), kind=kCustom, calls=%fused_computation.1.clone.1 | custom fusion | flops 524288 | bytes 6291584 | tf_op jit(solution)/shard_map/while/body/scatter-add | solution.py:35
  293.3 9.2 %convert_element_type.11 = bf16[256,128,128]{2,1,0:T(8,128)(2,1)} convert(f32[256,128,128]{2,1,0:T(8,128)} %get-tuple-element.48) | non-fusion elementwise | flops 4194304 | bytes 25165824 | tf_op jit(solution)/shard_map/convert_element_type | solution.py:40
  302.5 171.8 %reduce-scatter.2.cloned.1.call-done = bf16[2048,128]{1,0:T(8,128)(2,1)} async-done(((bf16[32768,128]{1,0:T(8,128)(2,1)}), bf16[2048,128]{1,0:T(8,128)(2,1)}) %reduce-scatter.2.cloned.1.call-update) | async-done | bytes 524304 | tf_op jit(solution)/shard_map/reduce_scatter | solution.py:43
  474.3 2.4 fusion.7
  (38 shorter events, 16.3 us)
Async XLA Ops:
  6.5 467.8 %copy-start = (bf16[128,256]{1,0:T(8,128)(2,1)S(1)}, bf16[128,256]{1,0:T(8,128)(2,1)}, u32[]{:S(2)}) copy-start(bf16[128,256]{1,0:T(8,128)(2,1)} %param.14) | copy-start | bytes 196612
  6.5 172.1 %all-gather.2.cloned.1.call-start = ((), (), s32[]{:S(2)}) async-start(), calls=%async_computation.2 | async-start | bytes 17301504 | tf_op jit(solution)/shard_map/all_gather | solution.py:12
  22.0 452.3 %reduce-scatter.2.cloned.1.call-start = ((), (), s32[]{:S(2)}) async-start(), calls=%async_computation.3 | async-start | bytes 8912896 | tf_op jit(solution)/shard_map/reduce_scatter | solution.py:43
  302.5 171.9 %copy-start.1 = (f32[256]{0:T(256)S(1)}, f32[256]{0:T(256)}, u32[]{:S(2)}) copy-start(f32[256]{0:T(256)} %param.15) | copy-start | bytes 3076
Sparse Core Ops, SparseCore 0:
  22.1 156.4 all-gather.1
  302.6 171.6 reduce-scatter.1
